TPU v7x, 256 devices: a whole 4x4x8 slice. The times are simulated.
256 devices in a mesh: rep: 2 (over core), shard: 128 (over x, z, y).
Axes of the slice: x: 4, y: 4, z: 8, core: 2. Of those that a mesh axis runs over, the one named last changes fastest.
Arguments:
- grad: bfloat16 [192, 512, 2048], P(None, 'shard'), may hold values from -6 to 6
- momentum: bfloat16 [192, 512, 2048], P(None, 'shard'), may hold values from -6 to 6
- owners: int32 [2, 128, 2], replicated, may hold values from 0 to 192, as said below
Outputs:
- new_momentum: bfloat16 [192, 512, 2048], P(None, 'shard')
- update: bfloat16 [192, 512, 2048], P(None, 'shard')
Inputs may be any that keep to these rules, and one draw needn't show every extreme that they name: `owners`: no matrix index appears twice. In each device's row of 2 slots the entries naming matrices come before the empty ones (value 192). In every draw some device has all 2 slots filled, and some matrices are named by no slot.
All inputs are finite; a program needn't handle non-finite values.
Results may differ from a plain program's by a relative error of at most 0.013.
Values may be sent and summed in bfloat16 or wider, within the bound.
A program may use at most 128 MiB of HBM per device.

v0:
```python
import math
import jax
import jax.numpy as jnp
from jax import lax
from jax.sharding import PartitionSpec as P

R = 512
C = 2048
ITERS = 3
coef_a = 3.4445
coef_b = -4.775
coef_c = 2.0315
mom_decay = 0.95


def newton_schulz(matrix):
    whole = matrix.astype(jnp.float32)
    norm_value = jnp.sqrt(jnp.sum(whole * whole))
    current = (whole / (norm_value + 1e-07)).astype(jnp.bfloat16)
    scaled = None
    for turn_index in range(ITERS):
        gram = lax.dot_general(
            current, current, (((1,), (1,)), ((), ())), preferred_element_type=jnp.float32
        ).astype(jnp.bfloat16)
        square = jnp.dot(gram, gram, preferred_element_type=jnp.float32)
        mixer = (coef_b * gram.astype(jnp.float32) + coef_c * square).astype(jnp.bfloat16)
        result = coef_a * current.astype(jnp.float32) + jnp.dot(
            mixer, current, preferred_element_type=jnp.float32
        )
        if turn_index + 1 < ITERS:
            current = result.astype(jnp.bfloat16)
        else:
            scaled = (0.2 * math.sqrt(max(R, C)) * result).astype(jnp.bfloat16)
    return scaled


def spread_lists(owners, matrix_count, replicas, shard_count):
    devices = replicas * shard_count
    entries = owners.reshape(-1)
    alive = entries < matrix_count
    ordinal = jnp.cumsum(alive.astype(jnp.int32)) - 1
    per_device = (matrix_count + devices - 1) // devices
    target = jnp.where(alive, ordinal, devices * per_device)
    packed = (
        jnp.full((devices * per_device + 1,), matrix_count, jnp.int32)
        .at[target]
        .set(entries)[: devices * per_device]
    )
    return packed.reshape(per_device, shard_count, replicas).transpose(2, 1, 0)


def place_rows(returned, chosen, matrix_count):
    local_rows = returned.shape[1] // chosen.shape[1]
    pieces = returned.reshape(chosen.shape[0] * chosen.shape[1], local_rows, returned.shape[2])
    target = chosen.reshape(-1)
    empty = jnp.zeros((matrix_count, local_rows, returned.shape[2]), jnp.bfloat16)
    return empty.at[target].set(pieces, mode="drop")


def body(grad, momentum, owners):
    fresh = mom_decay * momentum.astype(jnp.float32) + grad.astype(jnp.float32)
    new_momentum = fresh.astype(jnp.bfloat16)
    nesterov = (grad.astype(jnp.float32) + mom_decay * fresh).astype(jnp.bfloat16)
    matrix_count = grad.shape[0]
    local_rows = grad.shape[1]
    width = grad.shape[2]
    replicas = lax.axis_size("rep")
    shard_count = lax.axis_size("shard")
    my_rep = lax.axis_index("rep")
    table = spread_lists(owners, matrix_count, replicas, shard_count)
    slot_count = table.shape[2]
    mine = lax.dynamic_index_in_dim(table, my_rep, 0, keepdims=False)
    chosen = mine.T
    usable = chosen < matrix_count
    taken = jnp.take(nesterov, jnp.minimum(chosen, matrix_count - 1), axis=0)
    outgoing = jnp.where(usable[:, :, None, None], taken, jnp.zeros_like(taken))
    outgoing = outgoing.reshape(slot_count, shard_count * local_rows, width)
    finished = lax.map(
        newton_schulz, lax.all_to_all(outgoing, "shard", split_axis=1, concat_axis=1, tiled=True)
    )
    returned = lax.all_to_all(finished, "shard", split_axis=1, concat_axis=1, tiled=True)
    both = lax.all_gather(returned, "rep", axis=0, tiled=True)
    every_choice = table.transpose(0, 2, 1).reshape(replicas * slot_count, shard_count)
    update = place_rows(both, every_choice, matrix_count)
    return (new_momentum, update)


def solution(mesh):
    placed = (P(None, "shard", None), P(None, "shard", None), P())
    return jax.shard_map(
        body,
        mesh=mesh,
        in_specs=placed,
        out_specs=(P(None, "shard", None), P(None, "shard", None)),
        check_vma=False,
    )
```

profile of v0, /device:TPU:1, one launch (start us, length us, event | category | flops | bytes accessed | tf_op | source)
XLA Modules:
  0.0 297.5 jit_solution(2510085038544679176)
XLA Ops:
  7.2 0.0 all-gather.2.cloned.1.call-start
  7.2 0.7 fusion.27
  7.9 0.8 copy.21
  8.7 0.1 copy.20
  8.9 0.1 reshape.208
  9.0 0.3 reduce-window.9
  9.3 0.1 slice.10
  9.4 0.1 slice_reduce_fusion
  9.5 0.1 add_add_fusion
  9.6 0.2 copy.19
  9.8 0.2 lt.81
  10.0 0.1 reshape.221
  10.1 2.4 scatter_custom_fusion
  12.6 0.1 reshape.206
  12.7 0.2 fusion.18
  12.9 0.2 compare_reduce_fusion
  13.1 7.1 %fusion = (bf16[192,4,2048]{2,1,0:T(4,128)(2,1)S(1)}, bf16[192,4,2048]{2,1,0:T(4,128)(2,1)}) fusion(bf16[192,4,2048]{2,1,0:T(4,128)(2,1)} %param.3, bf16[192,4,2048]{2,1,0:T(4,128)(2,1)} %param.4), kind=kLoop, calls=%fused_computation.5 | loop fusion | flops 12582912 | bytes 12582912 | tf_op jit(solution)/shard_map/convert_element_type | solution.py:63
  20.2 3.5 %gather_fusion = bf16[128,4,2048]{2,1,0:T(4,128)(2,1)} fusion(bf16[192,4,2048]{2,1,0:T(4,128)(2,1)S(1)} %get-tuple-element.15, s32[1024]{0:T(1024)S(1)} %pad_clamp_fusion), kind=kCustom, calls=%fused_computation | custom fusion | bytes 4194816 | tf_op jit(solution)/shard_map/jit(_take)/gather | solution.py:75
  23.7 2.5 gather.7
  26.3 0.1 broadcast_in_dim.51
  26.4 0.1 broadcast_in_dim.52
  26.5 0.1 broadcast_in_dim.54
  26.6 0.1 broadcast_in_dim.55
  26.7 0.3 select_select_fusion
  27.0 5.2 %copy.32 = bf16[1,512,2048]{2,0,1:T(2,128)(2,1)} copy(bf16[1,512,2048]{2,1,0:T(8,128)(2,1)S(1)} %select_select_fusion) | data formatting | bytes 4194304 | tf_op jit(solution)/shard_map/jit(_where)/select_n | solution.py:76
  32.2 0.5 broadcast.218
  32.7 13.1 %reduce.9 = bf16[512,2048]{1,0:T(8,128)(2,1)S(1)} reduce(bf16[512,1,2048]{2,1,0:T(2,128)(2,1)} %bitcast.34, bf16[]{:T(256)} %broadcast.218), dimensions={1}, to_apply=%bitcast.31.reduce_sub_computation | reduce | bytes 4194306
  45.8 2.8 reshape.240
  48.7 65.8 %all_to_all.10 = bf16[128,2,4096]{2,1,0:T(2,128)(2,1)S(1)} all-to-all(bf16[128,2,4096]{2,1,0:T(2,128)(2,1)} %reshape.240), channel_id=1, replica_groups=mesh['rep'=2,'shard'=128] {'shard'}, dimensions={0} | all-to-all | bytes 4194304 | tf_op jit(solution)/shard_map/all_to_all | solution.py:79
  114.4 6.8 %reshape.241 = bf16[512,1,2048]{2,1,0:T(2,128)(2,1)} reshape(bf16[128,2,4096]{2,1,0:T(2,128)(2,1)S(1)} %all_to_all.10) | data formatting | bytes 4194304
  121.2 4.8 %fusion.2 = f32[]{:T(128)} fusion(bf16[1,512,2048]{2,0,1:T(2,128)(2,1)} %bitcast.32), kind=kLoop, calls=%fused_computation.9 | loop fusion | flops 3145727 | bytes 2097156 | tf_op jit(solution)/shard_map/while/body/eval_jaxpr/reduce_sum | solution.py:18
  126.7 3.8 %fusion.5 = bf16[512,2048]{1,0:T(8,128)(2,1)S(1)} fusion(f32[]{:T(128)S(6)} %add.96, bf16[1,512,2048]{2,0,1:T(2,128)(2,1)} %bitcast.33), kind=kLoop, calls=%fused_computation.15 | loop fusion | flops 3145728 | bytes 4194308 | tf_op jit(solution)/shard_map/while/body/eval_jaxpr/convert_element_type | solution.py:19
  130.5 1.3 convolution_convert_fusion.2
  131.8 2.9 add_convert_fusion.1
  134.6 0.0 copy-start.1
  134.7 3.6 %convolution_convert_fusion.1 = bf16[512,512]{1,0:T(8,128)(2,1)S(1)} fusion(bf16[512,2048]{1,0:T(8,128)(2,1)} %add_convert_fusion.1), kind=kOutput, calls=%fused_computation.27 | convolution fusion | flops 1074003968 | bytes 2621440 | tf_op jit(solution)/shard_map/while/body/eval_jaxpr/dot_general | solution.py:22
  138.3 0.0 copy-done.1
  138.3 2.9 add_convert_fusion
  141.2 3.5 %convolution_convert_fusion = bf16[512,512]{1,0:T(8,128)(2,1)S(1)} fusion(bf16[512,2048]{1,0:T(8,128)(2,1)} %add_convert_fusion), kind=kOutput, calls=%fused_computation.26 | convolution fusion | flops 1074003968 | bytes 2621440 | tf_op jit(solution)/shard_map/while/body/eval_jaxpr/dot_general | solution.py:22
  144.7 3.8 %fusion.4 = bf16[1,512,2048]{2,1,0:T(8,128)(2,1)S(1)} fusion(bf16[512,2048]{1,0:T(8,128)(2,1)} %add_convert_fusion, bf16[512,512]{1,0:T(8,128)(2,1)S(1)} %convolution_convert_fusion), kind=kOutput, calls=%fused_computation.14 | convolution fusion | flops 1348730880 | bytes 4718592 | tf_op jit(solution)/shard_map/while/body/eval_jaxpr/dot_general | solution.py:27
  148.5 5.4 %copy.31 = bf16[1,512,2048]{2,0,1:T(2,128)(2,1)} copy(bf16[1,512,2048]{2,1,0:T(8,128)(2,1)S(1)} %fusion.4) | data formatting | bytes 4194304 | tf_op jit(solution)/shard_map/while/body/jit(dynamic_update_index_in_dim)/broadcast_in_dim | solution.py:78
  153.9 13.1 %reduce.10 = bf16[512,2048]{1,0:T(8,128)(2,1)S(1)} reduce(bf16[512,1,2048]{2,1,0:T(2,128)(2,1)} %bitcast.35, bf16[]{:T(256)} %broadcast.218), dimensions={1}, to_apply=%bitcast.30.reduce_sub_computation | reduce | bytes 4194306
  167.0 2.8 reshape.242
  169.9 58.7 %all_to_all.11 = bf16[128,2,4096]{2,1,0:T(2,128)(2,1)S(1)} all-to-all(bf16[128,2,4096]{2,1,0:T(2,128)(2,1)} %reshape.242), channel_id=1, replica_groups=mesh['rep'=2,'shard'=128] {'shard'}, dimensions={0} | all-to-all | bytes 4194304 | tf_op jit(solution)/shard_map/all_to_all | solution.py:81
  228.6 6.8 %reshape.243 = bf16[512,1,2048]{2,1,0:T(2,128)(2,1)} reshape(bf16[128,2,4096]{2,1,0:T(2,128)(2,1)S(1)} %all_to_all.11) | data formatting | bytes 4194304
  235.3 4.8 %copy.26 = bf16[1,512,2048]{2,1,0:T(8,128)(2,1)} copy(bf16[1,512,2048]{2,0,1:T(2,128)(2,1)} %bitcast.36) | data formatting | bytes 4194304 | tf_op jit(solution)/shard_map/all_to_all | solution.py:81
  240.1 0.0 all-gather.2.cloned.1.call-update
  240.1 0.1 copy.22
  240.2 17.8 %all-gather.2.cloned.1.call-done = bf16[2,512,2048]{2,1,0:T(8,128)(2,1)} async-done(((bf16[1,512,2048]{2,1,0:T(8,128)(2,1)}), bf16[2,512,2048]{2,1,0:T(8,128)(2,1)}) %all-gather.2.cloned.1.call-update) | async-done | bytes 4194320 | tf_op jit(solution)/shard_map/all_gather | solution.py:82
  258.0 7.2 %reshape.229 = bf16[256,4,2048]{2,1,0:T(4,128)(2,1)} reshape(bf16[2,512,2048]{2,1,0:T(8,128)(2,1)} %all-gather.2.cloned.1.call-done) | data formatting | bytes 8388608 | tf_op jit(solution)/shard_map/reshape | solution.py:54
  265.2 1.6 broadcast_in_dim.48
  266.8 22.2 %scatter_fusion = bf16[192,4,2048]{2,1,0:T(4,128)(2,1)S(1)} fusion(bf16[192,4,2048]{2,1,0:T(4,128)(2,1)S(1)} %broadcast_in_dim.48, s32[256]{0:T(256)S(1)} %bitcast.39, bf16[256,4,2048]{2,1,0:T(4,128)(2,1)} %reshape.229), kind=kCustom, calls=%fused_computation.2 | custom fusion | bytes 12583936 | tf_op jit(solution)/shard_map/scatter | solution.py:57
  289.0 0.0 copy-start
  289.0 1.7 copy-done
  (5 shorter events, 0.1 us)
Async XLA Ops:
  7.2 250.8 %all-gather.2.cloned.1.call-start = ((), (), s32[]{:S(2)}) async-start(), calls=%async_computation.2 | async-start | bytes 6291456 | tf_op jit(solution)/shard_map/all_gather | solution.py:82
  134.6 3.7 %copy-start.1 = (bf16[512,2048]{1,0:T(8,128)(2,1)S(1)}, bf16[512,2048]{1,0:T(8,128)(2,1)}, u32[]{:S(2)}) copy-start(bf16[512,2048]{1,0:T(8,128)(2,1)} %add_convert_fusion.1) | copy-start | bytes 6291460
  289.0 1.7 copy-start
Sparse Core Ops, SparseCore 0:
  240.3 17.6 all-gather.1
where the time goes:
time: 299 us; the launch traced here: 298 us
  blocking collectives  124 us (41%)
  local copies, waits for them, and re-layouts  78.6 us (26%)
  other arithmetic  43.7 us (15%)
  matrix products  18 us (6%)
  waiting for transfers between devices  17.8 us (6%)
  between operations  14.9 us (5%)
    all_to_all x1, blocking collectives, body(): lax.all_to_all(outgoing, 'shard', split_axis=1, concat_axis=1, tiled=True)  65.8 us
    all_to_all x1, blocking collectives, body(): lax.all_to_all(finished, 'shard', split_axis=1, concat_axis=1, tiled=True)  58.7 us
    unnamed x2, other arithmetic  26.2 us
    scatter x1, local copies, waits for them, and re-layouts, place_rows(): return empty.at[target].set(pieces, mode='drop')  22.2 us
    unnamed x10, local copies, waits for them, and re-layouts  22.2 us
    all_gather x1, waiting for transfers between devices, body(): both = lax.all_gather(returned, 'rep', axis=0, tiled=True)  17.8 us
    dot_general x3, matrix products, newton_schulz(): jnp.dot(mixer, current, preferred_element_type=jnp.float32)  9.57 us
    dot_general x3, matrix products, newton_schulz(): lax.dot_general(current, current, (((1,), (1,)), ((), ())), preferred_ele...  8.43 us
  transfers between devices with their start and end apart: 1, of which 1 were waited for; matrix products, arithmetic and copies ran while one was open for 0% of the time, Pallas kernels for 0%

commit v1 on v0

--- a/solution.py
+++ b/solution.py
@@ -1,3 +1,4 @@
+import functools
 import math
 import jax
 import jax.numpy as jnp
@@ -11,6 +12,15 @@
 coef_b = -4.775
 coef_c = 2.0315
 mom_decay = 0.95
+
+
+def compute_region(x_part, link_axis):
+    earlier = jnp.stack(jnp.split(x_part, jax.lax.axis_size(link_axis), axis=1))
+    latest = jax.lax.all_to_all(earlier, link_axis, 0, 0)
+    return jnp.concatenate(latest, axis=1)
+
+
+_point_column = functools.partial(compute_region, link_axis="shard")
 
 
 def newton_schulz(matrix):
@@ -78,7 +88,7 @@
     finished = lax.map(
         newton_schulz, lax.all_to_all(outgoing, "shard", split_axis=1, concat_axis=1, tiled=True)
     )
-    returned = lax.all_to_all(finished, "shard", split_axis=1, concat_axis=1, tiled=True)
+    returned = _point_column(finished)
     both = lax.all_gather(returned, "rep", axis=0, tiled=True)
     every_choice = table.transpose(0, 2, 1).reshape(replicas * slot_count, shard_count)
     update = place_rows(both, every_choice, matrix_count)

time: 299 us -> 271 us (0.906)
  local copies, waits for them, and re-layouts: 78.6 us -> 63.3 us
  other arithmetic: 43.7 us -> 30.7 us
    unnamed x2 -> x1, other arithmetic: 26.2 us -> 13.2 us
    unnamed x10 -> x135, local copies, waits for them, and re-layouts: 22.2 us -> 15 us
    broadcast_in_dim x1 -> x0, local copies, waits for them, and re-layouts: 5.38 us -> none  [body(): lax.map(newton_schulz, lax.all_to_all(outgoing, 'shard', split_axis=1, co...]
    all_to_all x1 -> x0, local copies, waits for them, and re-layouts: 4.78 us -> none  [body(): lax.all_to_all(finished, 'shard', split_axis=1, concat_axis=1, tiled=True)]
where the time goes in v1:
time: 271 us; the launch traced here: 270 us
  blocking collectives  124 us (46%)
  local copies, waits for them, and re-layouts  63.3 us (23%)
  other arithmetic  30.7 us (11%)
  matrix products  18 us (7%)
  waiting for transfers between devices  17.8 us (7%)
  between operations  15.5 us (6%)
    all_to_all x1, blocking collectives, body(): lax.all_to_all(outgoing, 'shard', split_axis=1, concat_axis=1, tiled=True)  65.8 us
    all_to_all x1, blocking collectives, compute_region(): latest = jax.lax.all_to_all(earlier, link_axis, 0, 0)  58.5 us
    scatter x1, local copies, waits for them, and re-layouts, place_rows(): return empty.at[target].set(pieces, mode='drop')  22.2 us
    all_gather x1, waiting for transfers between devices, body(): both = lax.all_gather(returned, 'rep', axis=0, tiled=True)  17.8 us
    unnamed x135, local copies, waits for them, and re-layouts  15 us
    unnamed x1, other arithmetic  13.2 us
    dot_general x3, matrix products, newton_schulz(): jnp.dot(mixer, current, preferred_element_type=jnp.float32)  9.56 us
    dot_general x3, matrix products, newton_schulz(): lax.dot_general(current, current, (((1,), (1,)), ((), ())), preferred_ele...  8.43 us
  transfers between devices with their start and end apart: 1, of which 1 were waited for; matrix products, arithmetic and copies ran while one was open for 0% of the time, Pallas kernels for 0%

profile of v1, /device:TPU:1, one launch (start us, length us, event | category | flops | bytes accessed | tf_op | source)
XLA Modules:
  0.0 269.5 jit_solution(8175058781972107704)
XLA Ops:
  7.2 0.0 all-gather.2.cloned.1.call-start
  7.2 0.7 fusion.27
  7.9 0.8 copy.19
  8.7 0.1 copy.18
  8.9 0.1 reshape.212
  9.0 0.3 reduce-window.9
  9.3 0.1 slice.10
  9.4 0.1 slice_reduce_fusion
  9.5 0.1 add_add_fusion
  9.6 0.2 copy.17
  9.8 0.2 lt.81
  10.0 0.1 reshape.225
  10.1 2.4 scatter_custom_fusion
  12.6 0.1 reshape.209
  12.7 0.2 fusion.18
  12.9 0.2 compare_reduce_fusion
  13.1 7.1 %fusion = (bf16[192,4,2048]{2,1,0:T(4,128)(2,1)S(1)}, bf16[192,4,2048]{2,1,0:T(4,128)(2,1)}) fusion(bf16[192,4,2048]{2,1,0:T(4,128)(2,1)} %param.3, bf16[192,4,2048]{2,1,0:T(4,128)(2,1)} %param.4), kind=kLoop, calls=%fused_computation.5 | loop fusion | flops 12582912 | bytes 12582912 | tf_op jit(solution)/shard_map/convert_element_type | solution.py:73
  20.2 3.5 %gather_fusion = bf16[128,4,2048]{2,1,0:T(4,128)(2,1)} fusion(bf16[192,4,2048]{2,1,0:T(4,128)(2,1)S(1)} %get-tuple-element.15, s32[1024]{0:T(1024)S(1)} %pad_clamp_fusion), kind=kCustom, calls=%fused_computation | custom fusion | bytes 4194816 | tf_op jit(solution)/shard_map/jit(_take)/gather | solution.py:85
  23.7 2.5 gather.7
  26.3 0.1 broadcast_in_dim.51
  26.4 0.1 broadcast_in_dim.52
  26.5 0.1 broadcast_in_dim.54
  26.6 0.1 broadcast_in_dim.55
  26.7 0.3 select_select_fusion
  27.0 5.2 %copy.26 = bf16[1,512,2048]{2,0,1:T(2,128)(2,1)} copy(bf16[1,512,2048]{2,1,0:T(8,128)(2,1)S(1)} %select_select_fusion) | data formatting | bytes 4194304 | tf_op jit(solution)/shard_map/jit(_where)/select_n | solution.py:86
  32.2 0.5 broadcast.218
  32.7 13.2 %reduce.9 = bf16[512,2048]{1,0:T(8,128)(2,1)S(1)} reduce(bf16[512,1,2048]{2,1,0:T(2,128)(2,1)} %bitcast.542, bf16[]{:T(256)} %broadcast.218), dimensions={1}, to_apply=%bitcast.539.reduce_sub_computation | reduce | bytes 4194306
  45.9 2.8 %reshape.244 = bf16[128,2,4096]{2,1,0:T(2,128)(2,1)} reshape(bf16[512,2048]{1,0:T(8,128)(2,1)S(1)} %reduce.9) | data formatting | bytes 4194304
  48.7 65.8 %all_to_all.10 = bf16[128,2,4096]{2,1,0:T(2,128)(2,1)S(1)} all-to-all(bf16[128,2,4096]{2,1,0:T(2,128)(2,1)} %reshape.244), channel_id=1, replica_groups=mesh['rep'=2,'shard'=128] {'shard'}, dimensions={0} | all-to-all | bytes 4194304 | tf_op jit(solution)/shard_map/all_to_all | solution.py:89
  114.5 6.8 %reshape.245 = bf16[512,1,2048]{2,1,0:T(2,128)(2,1)} reshape(bf16[128,2,4096]{2,1,0:T(2,128)(2,1)S(1)} %all_to_all.10) | data formatting | bytes 4194304
  121.2 4.8 %fusion.2 = f32[]{:T(128)} fusion(bf16[1,512,2048]{2,0,1:T(2,128)(2,1)} %bitcast.540), kind=kLoop, calls=%fused_computation.9 | loop fusion | flops 3145727 | bytes 2097156 | tf_op jit(solution)/shard_map/while/body/eval_jaxpr/reduce_sum | solution.py:28
  126.7 3.8 %fusion.5 = bf16[512,2048]{1,0:T(8,128)(2,1)S(1)} fusion(f32[]{:T(128)S(6)} %add.96, bf16[1,512,2048]{2,0,1:T(2,128)(2,1)} %bitcast.541), kind=kLoop, calls=%fused_computation.15 | loop fusion | flops 3145728 | bytes 4194308 | tf_op jit(solution)/shard_map/while/body/eval_jaxpr/convert_element_type | solution.py:29
  130.5 1.3 convolution_convert_fusion.2
  131.8 2.9 %add_convert_fusion.1 = bf16[512,2048]{1,0:T(8,128)(2,1)} fusion(bf16[512,2048]{1,0:T(8,128)(2,1)S(1)} %fusion.5, bf16[512,512]{1,0:T(8,128)(2,1)S(1)} %convolution_convert_fusion.2), kind=kOutput, calls=%fused_computation.13 | convolution fusion | flops 1347682304 | bytes 4718592 | tf_op jit(solution)/shard_map/while/body/eval_jaxpr/dot_general | solution.py:37
  134.7 0.0 copy-start.1
  134.7 3.6 %convolution_convert_fusion.1 = bf16[512,512]{1,0:T(8,128)(2,1)S(1)} fusion(bf16[512,2048]{1,0:T(8,128)(2,1)} %add_convert_fusion.1), kind=kOutput, calls=%fused_computation.27 | convolution fusion | flops 1074003968 | bytes 2621440 | tf_op jit(solution)/shard_map/while/body/eval_jaxpr/dot_general | solution.py:32
  138.3 0.0 copy-done.1
  138.3 2.9 %add_convert_fusion = bf16[512,2048]{1,0:T(8,128)(2,1)} fusion(bf16[512,2048]{1,0:T(8,128)(2,1)S(1)} %copy-done.1, bf16[512,512]{1,0:T(8,128)(2,1)S(1)} %convolution_convert_fusion.1), kind=kOutput, calls=%fused_computation.12 | convolution fusion | flops 1347682304 | bytes 4718592 | tf_op jit(solution)/shard_map/while/body/eval_jaxpr/dot_general | solution.py:37
  141.2 3.5 %convolution_convert_fusion = bf16[512,512]{1,0:T(8,128)(2,1)S(1)} fusion(bf16[512,2048]{1,0:T(8,128)(2,1)} %add_convert_fusion), kind=kOutput, calls=%fused_computation.26 | convolution fusion | flops 1074003968 | bytes 2621440 | tf_op jit(solution)/shard_map/while/body/eval_jaxpr/dot_general | solution.py:32
  144.7 3.8 %fusion.4 = bf16[1,512,2048]{2,1,0:T(8,128)(2,1)S(1)} fusion(bf16[512,2048]{1,0:T(8,128)(2,1)} %add_convert_fusion, bf16[512,512]{1,0:T(8,128)(2,1)S(1)} %convolution_convert_fusion), kind=kOutput, calls=%fused_computation.14 | convolution fusion | flops 1348730880 | bytes 4718592 | tf_op jit(solution)/shard_map/while/body/eval_jaxpr/dot_general | solution.py:37
  149.9 0.2 constant_dynamic-update-slice_fusion.67
  151.6 58.5 %all_to_all.11 = bf16[128,1,4,2048]{3,2,1,0:T(4,128)(2,1)S(1)} all-to-all(bf16[128,1,4,2048]{3,2,1,0:T(4,128)(2,1)S(1)} %constant_dynamic-update-slice_fusion), channel_id=1, replica_groups=mesh['rep'=2,'shard'=128] {'shard'}, dimensions={0} | all-to-all | bytes 4194304 | tf_op jit(solution)/shard_map/all_to_all | solution.py:19
  210.1 2.0 reshape.210
  212.1 0.0 all-gather.2.cloned.1.call-update
  212.1 0.1 copy.20
  212.2 17.8 %all-gather.2.cloned.1.call-done = bf16[2,512,2048]{2,1,0:T(8,128)(2,1)} async-done(((bf16[1,512,2048]{2,1,0:T(8,128)(2,1)}), bf16[2,512,2048]{2,1,0:T(8,128)(2,1)}) %all-gather.2.cloned.1.call-update) | async-done | bytes 4194320 | tf_op jit(solution)/shard_map/all_gather | solution.py:92
  230.0 7.2 %reshape.233 = bf16[256,4,2048]{2,1,0:T(4,128)(2,1)} reshape(bf16[2,512,2048]{2,1,0:T(8,128)(2,1)} %all-gather.2.cloned.1.call-done) | data formatting | bytes 8388608 | tf_op jit(solution)/shard_map/reshape | solution.py:64
  237.2 1.6 broadcast_in_dim.48
  238.8 22.2 %scatter_fusion = bf16[192,4,2048]{2,1,0:T(4,128)(2,1)S(1)} fusion(bf16[192,4,2048]{2,1,0:T(4,128)(2,1)S(1)} %broadcast_in_dim.48, s32[256]{0:T(256)S(1)} %bitcast.545, bf16[256,4,2048]{2,1,0:T(4,128)(2,1)} %reshape.233), kind=kCustom, calls=%fused_computation.2 | custom fusion | bytes 12583936 | tf_op jit(solution)/shard_map/scatter | solution.py:67
  261.0 0.0 copy-start
  261.0 1.7 copy-done
  (132 shorter events, 2.3 us)
Async XLA Ops:
  7.2 222.8 %all-gather.2.cloned.1.call-start = ((), (), s32[]{:S(2)}) async-start(), calls=%async_computation.2 | async-start | bytes 6291456 | tf_op jit(solution)/shard_map/all_gather | solution.py:92
  134.7 3.7 %copy-start.1 = (bf16[512,2048]{1,0:T(8,128)(2,1)S(1)}, bf16[512,2048]{1,0:T(8,128)(2,1)}, u32[]{:S(2)}) copy-start(bf16[512,2048]{1,0:T(8,128)(2,1)} %add_convert_fusion.1) | copy-start | bytes 6291460
  261.0 1.7 copy-start
Sparse Core Ops, SparseCore 0:
  212.3 17.6 all-gather.1
